TPU v7x, 256 devices: a whole 4x4x8 slice. The times are simulated.
256 devices in a mesh: wide: 16 (over z_lo, x, core), long: 16 (over y, z_hi).
Axes of the slice: x: 4, y: 4, z: 8 (z_hi: 4, z_lo: 2; z = z_hi * 2 + z_lo), core: 2. Of those that a mesh axis runs over, the one named last changes fastest.
Arguments:
- slab_vertices: float32 [3, 4096], P(None, 'wide'), may hold values from 0 to 1
- slab_elements: int32 [3, 8192], P(None, 'wide'), may hold values from 0 to 4095, as said below
- source_vertices: float32 [3, 16384], P(None, ('wide', 'long')), may hold values from 0 to 1
- source_elements: int32 [3, 32768], P(None, ('wide', 'long')), may hold values from 0 to 16383, as said below
- primal_basis: bfloat16 [32, 32768], P(None, ('wide', 'long')), may hold values from -12 to 12
- adjoint_basis: bfloat16 [32, 8192], P(None, 'wide'), may hold values from -24 to 24
Outputs:
- primal_image: float32 [32, 8192], P(None, ('wide', 'long'))
- adjoint_image: float32 [32, 32768], P(None, ('wide', 'long'))
Inputs may be any that keep to these rules, and one draw needn't show every extreme that they name: `slab_elements`: a slab triangle in columns b * 512 to (b + 1) * 512 - 1 names only vertices b * 256 to (b + 1) * 256 - 1; both ends of each such range are named. `source_elements`: a source triangle in columns b * 128 to (b + 1) * 128 - 1 names only vertices b * 64 to (b + 1) * 64 - 1; both ends of each such range are named.
All inputs are finite; a program needn't handle non-finite values.
Results may differ from a plain program's by a relative error of at most 0.0029.
Values may be sent and summed in bfloat16 or wider, within the bound.
A program may use at most 64 MiB of HBM per device.

v0:
```python
import math
import jax
import jax.numpy as jnp
from jax import lax
from jax.sharding import PartitionSpec as P

WAVENUMBER = 40.0
SOFTENING = 0.0004
AREA_WEIGHT = 0.05
FOUR_PI = 4.0 * math.pi


def geometry(vertices, elements, anchor):
    local_ids = elements - anchor
    corners = [jnp.take(vertices, local_ids[corner], axis=1) for corner in range(3)]
    centre = (corners[0] + corners[1] + corners[2]) / 3.0
    edge_one = corners[1] - corners[0]
    edge_two = corners[2] - corners[0]
    normal_x = edge_one[1] * edge_two[2] - edge_one[2] * edge_two[1]
    normal_y = edge_one[2] * edge_two[0] - edge_one[0] * edge_two[2]
    normal_z = edge_one[0] * edge_two[1] - edge_one[1] * edge_two[0]
    areas = 0.5 * jnp.sqrt(normal_x * normal_x + normal_y * normal_y + normal_z * normal_z)
    return jnp.concatenate([centre, areas[None, :]], axis=0)


def kernel_tile(targets, sources):
    spread = targets[0][:, None] - sources[0][None, :]
    square_sum = spread * spread
    for axis_id in range(1, 3):
        spread = targets[axis_id][:, None] - sources[axis_id][None, :]
        square_sum = square_sum + spread * spread
    radius = jnp.sqrt(
        square_sum + SOFTENING + AREA_WEIGHT * (targets[3][:, None] + sources[3][None, :])
    )
    weight = targets[3][:, None] * sources[3][None, :] / (FOUR_PI * radius)
    phases = WAVENUMBER * radius
    return (
        (weight * jnp.cos(phases)).astype(jnp.bfloat16),
        (weight * jnp.sin(phases)).astype(jnp.bfloat16),
    )


def pack_primal(columns):
    half_rows = columns.shape[0] // 2
    real_part = columns[:half_rows]
    imag_part = columns[half_rows:]
    return jnp.concatenate(
        [jnp.concatenate([real_part, -imag_part], 1), jnp.concatenate([imag_part, real_part], 1)], 0
    )


def pack_adjoint(row_block):
    half_rows = row_block.shape[0] // 2
    real_part = row_block[:half_rows]
    imag_part = row_block[half_rows:]
    return jnp.concatenate(
        [jnp.concatenate([real_part, imag_part], 1), jnp.concatenate([imag_part, -real_part], 1)], 0
    )


def primal_part(primal_pack, tile_real, tile_imag):
    stacked = jnp.concatenate([tile_real, tile_imag], 1)
    return lax.dot_general(
        primal_pack, stacked, (((1,), (1,)), ((), ())), preferred_element_type=jnp.float32
    )


def adjoint_part(adjoint_pack, tile_real, tile_imag):
    stacked = jnp.concatenate([tile_real, tile_imag], 0)
    return jnp.dot(adjoint_pack, stacked, preferred_element_type=jnp.float32)


def shards(
    slab_vertices, slab_elements, source_vertices, source_elements, primal_basis, adjoint_basis
):
    slab_width = slab_elements.shape[1]
    source_width = source_elements.shape[1]
    wide_at = lax.axis_index("wide")
    flat_at = wide_at * lax.axis_size("long") + lax.axis_index("long")
    slab_points = geometry(slab_vertices, slab_elements, wide_at * (slab_width // 2))
    source_points = geometry(source_vertices, source_elements, flat_at * (source_width // 2))
    gathered_points = lax.all_gather(source_points, "wide", axis=1, tiled=True)
    gathered_basis = lax.all_gather(primal_basis, "wide", axis=1, tiled=True)
    tile_real, tile_imag = kernel_tile(slab_points, gathered_points)
    primal_acc = primal_part(pack_primal(gathered_basis), tile_real, tile_imag)
    adjoint_acc = adjoint_part(pack_adjoint(adjoint_basis), tile_real, tile_imag)
    primal_image = lax.psum_scatter(primal_acc, "long", scatter_dimension=1, tiled=True)
    adjoint_image = lax.psum_scatter(adjoint_acc, "wide", scatter_dimension=1, tiled=True)
    return (primal_image, adjoint_image)


def solution(mesh):
    return jax.shard_map(
        shards,
        mesh=mesh,
        in_specs=(
            P(None, "wide"),
            P(None, "wide"),
            P(None, ("wide", "long")),
            P(None, ("wide", "long")),
            P(None, ("wide", "long")),
            P(None, "wide"),
        ),
        out_specs=(P(None, ("wide", "long")), P(None, ("wide", "long"))),
        check_vma=False,
    )
```

profile of v0, /device:TPU:8, one launch (start us, length us, event | category | flops | bytes accessed | tf_op | source)
XLA Modules:
  0.0 232.3 jit_solution(14007705249488354865)
XLA Ops:
  7.2 0.0 reduce-scatter.7.cloned.1.call-start
  7.2 0.7 broadcast_subtract_fusion
  8.0 0.8 copy.35
  8.8 0.7 broadcast_subtract_fusion.1
  9.5 0.6 gather_fusion.5
  10.1 0.1 copy.40
  10.2 0.7 gather_fusion.4
  10.9 0.1 copy.38
  10.9 0.7 gather_fusion.3
  11.6 0.1 copy.36
  11.7 20.1 %all_gather.7 = f32[4,2048]{1,0:T(4,128)S(1)} all-gather(f32[4,128]{1,0:T(4,128)S(1)} %pad_maximum_fusion), channel_id=1, replica_groups=mesh['wide'=16,'long'=16] {'wide'}, dimensions={1}, use_global_device_ids=true | all-gather | bytes 34816 | tf_op jit(solution)/shard_map/all_gather | solution.py:82
  31.8 0.8 copy.29
  32.7 1.0 gather_fusion.2
  33.7 0.1 copy.34
  33.8 1.0 gather_fusion.1
  34.9 0.1 copy.32
  35.0 1.0 gather_fusion
  36.1 0.1 copy.30
  36.2 16.9 %all_gather.6 = bf16[32,2048]{1,0:T(8,128)(2,1)S(1)} all-gather(bf16[32,128]{1,0:T(8,128)(2,1)} %param.14), channel_id=1, replica_groups=mesh['wide'=16,'long'=16] {'wide'}, dimensions={1}, use_global_device_ids=true | all-gather | bytes 139264 | tf_op jit(solution)/shard_map/all_gather | solution.py:83
  53.1 19.3 %multiply_convert_fusion.1 = (bf16[512,2048]{1,0:T(8,128)(2,1)S(1)}, bf16[512,2048]{1,0:T(8,128)(2,1)S(1)}) fusion(f32[2048]{0:T(1024)S(1)} %bitcast.59, f32[512]{0:T(512)S(1)} %bitcast.64, f32[2048]{0:T(1024)S(1)} %bitcast.60, f32[512]{0:T(512)S(1)} %bitcast.65, f32[2048]{0:T(1024)S(1)} %bitcast.61, f32[512]{0:T(512)S(1)} %bitcast.63, ...), kind=kLoop, calls=%fused_computation.15 | loop fusion | flops 20971520 | bytes 4235264 | tf_op jit(solution)/shard_map/convert_element_type | solution.py:38
  72.4 0.0 copy-start.1
  72.4 1.3 copy-done.1
  73.7 0.0 copy-start
  73.7 1.9 fusion.8
  75.6 0.0 reduce-scatter.7.cloned.1.call-update
  75.6 0.0 reduce-scatter.5.cloned.1.call-start
  75.7 0.0 copy-done
  75.7 3.1 %fusion.4 = f32[32,2048]{1,0:T(8,128)} fusion(bf16[512,2048]{1,0:T(8,128)(2,1)} %copy-done.1, bf16[512,2048]{1,0:T(8,128)(2,1)S(1)} %get-tuple-element.13, bf16[16,512]{1,0:T(8,128)(2,1)S(1)} %get-tuple-element.16, bf16[16,512]{1,0:T(8,128)(2,1)S(1)} %get-tuple-element.17, bf16[16,512]{1,0:T(8,128)(2,1)S(1)} %get-tuple-element.15), kind=kOutput, calls=%fused_computation.10 | convolution fusion | flops 142868480 | bytes 4505600 | tf_op jit(solution)/shard_map/dot_general | solution.py:70
  78.8 0.0 reduce-scatter.5.cloned.1.call-update
  78.9 82.1 %reduce-scatter.7.cloned.1.call-done = f32[32,32]{1,0:T(8,128)} async-done(((f32[512,32]{1,0:T(8,128)}), f32[32,32]{1,0:T(8,128)}) %reduce-scatter.7.cloned.1.call-update) | async-done | bytes 4112
  161.0 1.4 copy.42
  162.3 63.1 %reduce-scatter.5.cloned.1.call-done = f32[32,128]{1,0:T(8,128)} async-done(((f32[32,2048]{1,0:T(8,128)}), f32[32,128]{1,0:T(8,128)}) %reduce-scatter.5.cloned.1.call-update) | async-done | bytes 16400 | tf_op jit(solution)/shard_map/reduce_scatter | solution.py:88
  (21 shorter events, 0.2 us)
Async XLA Ops:
  7.2 153.8 %reduce-scatter.7.cloned.1.call-start = ((), (), s32[]{:S(2)}) async-start(), calls=%async_computation.3 | async-start | bytes 278528
  72.4 1.3 copy-start.1
  73.7 2.0 copy-start
  75.6 149.8 %reduce-scatter.5.cloned.1.call-start = ((), (), s32[]{:S(2)}) async-start(), calls=%async_computation.2 | async-start | bytes 278528 | tf_op jit(solution)/shard_map/reduce_scatter | solution.py:88
Sparse Core Ops, SparseCore 0:
  75.8 85.1 reduce-scatter.6
  164.2 61.2 reduce-scatter.4
where the time goes:
time: 233 us; the launch traced here: 232 us
  waiting for transfers between devices  145 us (62%)
  blocking collectives  37 us (16%)
  other arithmetic  20.8 us (9%)
  between operations  14.2 us (6%)
  local copies, waits for them, and re-layouts  9.95 us (4%)
  matrix products  5.05 us (2%)
    unnamed x3, waiting for transfers between devices  82.1 us
    reduce_scatter x1, waiting for transfers between devices, shards(): lax.psum_scatter(adjoint_acc, 'wide', scatter_dimension=1, tiled=True)  63.1 us
    all_gather x1, blocking collectives, shards(): gathered_points = lax.all_gather(source_points, 'wide', axis=1, tiled=True)  20.1 us
    convert_element_type x1, other arithmetic, kernel_tile(): (weight * jnp.cos(phases)).astype(jnp.bfloat16)  19.3 us
    all_gather x1, blocking collectives, shards(): gathered_basis = lax.all_gather(primal_basis, 'wide', axis=1, tiled=True)  16.9 us
    gather x12, local copies, waits for them, and re-layouts, geometry(): jnp.take(vertices, local_ids[corner], axis=1)  5.6 us
  transfers between devices with their start and end apart: 2, of which 2 were waited for; matrix products, arithmetic and copies ran while one was open for 2% of the time, Pallas kernels for 0%

commit v1 on v0

--- a/solution.py
+++ b/solution.py
@@ -79,7 +79,9 @@
     flat_at = wide_at * lax.axis_size("long") + lax.axis_index("long")
     slab_points = geometry(slab_vertices, slab_elements, wide_at * (slab_width // 2))
     source_points = geometry(source_vertices, source_elements, flat_at * (source_width // 2))
-    gathered_points = lax.all_gather(source_points, "wide", axis=1, tiled=True)
+    gathered_points = jnp.concatenate(
+        lax.all_to_all(jnp.stack([source_points] * lax.axis_size("wide")), "wide", 0, 0), axis=1
+    )
     gathered_basis = lax.all_gather(primal_basis, "wide", axis=1, tiled=True)
     tile_real, tile_imag = kernel_tile(slab_points, gathered_points)
     primal_acc = primal_part(pack_primal(gathered_basis), tile_real, tile_imag)

time: 233 us -> 222 us (0.953)
  blocking collectives: 37 us -> 20.5 us
  starting transfers between devices: 0.08 us -> 5.84 us
    all_gather x1 -> x0, blocking collectives: 20.1 us -> none  [shards(): gathered_points = lax.all_gather(source_points, 'wide', axis=1, tiled=True)]
    all_to_all x0 -> x1, starting transfers between devices: none -> 5.76 us  [shards(): lax.all_to_all(jnp.stack([source_points] * lax.axis_size('wide')), 'wide'...]
    all_gather x1, blocking collectives: 16.9 us -> 20.5 us  [shards(): gathered_basis = lax.all_gather(primal_basis, 'wide', axis=1, tiled=True)]
  transfers between devices with their start and end apart: 2 -> 3, of which waited for: 2 -> 2; matrix products, arithmetic and copies ran while one was open for 2% -> 4% of each run, Pallas kernels for 0% -> 0%
where the time goes in v1:
time: 222 us; the launch traced here: 221 us
  waiting for transfers between devices  144 us (65%)
  other arithmetic  20.8 us (9%)
  blocking collectives  20.5 us (9%)
  between operations  14.2 us (6%)
  local copies, waits for them, and re-layouts  10.6 us (5%)
  starting transfers between devices  5.84 us (3%)
  matrix products  5.07 us (2%)
    unnamed x3, waiting for transfers between devices  81.2 us
    reduce_scatter x1, waiting for transfers between devices, shards(): lax.psum_scatter(adjoint_acc, 'wide', scatter_dimension=1, tiled=True)  62.9 us
    all_gather x1, blocking collectives, shards(): gathered_basis = lax.all_gather(primal_basis, 'wide', axis=1, tiled=True)  20.5 us
    convert_element_type x1, other arithmetic, kernel_tile(): (weight * jnp.cos(phases)).astype(jnp.bfloat16)  19.3 us
    all_to_all x1, starting transfers between devices, shards(): lax.all_to_all(jnp.stack([source_points] * lax.axis_size('wide')), 'wide'...  5.76 us
    gather x12, local copies, waits for them, and re-layouts, geometry(): jnp.take(vertices, local_ids[corner], axis=1)  5.6 us
  transfers between devices with their start and end apart: 3, of which 2 were waited for; matrix products, arithmetic and copies ran while one was open for 4% of the time, Pallas kernels for 0%

profile of v1, /device:TPU:8, one launch (start us, length us, event | category | flops | bytes accessed | tf_op | source)
XLA Modules:
  0.0 221.1 jit_solution(3437253569537557720)
XLA Ops:
  7.2 0.8 copy.37
  8.0 0.7 broadcast_subtract_fusion.1
  8.7 0.6 gather_fusion.5
  9.3 0.1 copy.42
  9.4 0.7 gather_fusion.4
  10.0 0.1 copy.40
  10.1 0.7 gather_fusion.3
  10.8 0.1 copy.38
  10.9 0.6 stack.2
  11.5 5.8 %all-to-all-start = ((f32[16,4,128]{2,1,0:T(4,128)}), f32[16,4,128]{2,1,0:T(4,128)S(1)}, u32[]{:S(2)}, u32[]{:S(2)}) async-start(f32[16,4,128]{2,1,0:T(4,128)} %stack.2), calls=%async_computation | async-start | bytes 65536 | tf_op jit(solution)/shard_map/all_to_all | solution.py:83
  17.3 0.0 reduce-scatter.7.cloned.1.call-start
  17.3 0.7 broadcast_subtract_fusion
  18.1 0.8 copy.31
  19.0 1.0 gather_fusion.2
  20.0 0.1 copy.36
  20.1 1.0 gather_fusion.1
  21.2 0.1 copy.34
  21.3 1.0 gather_fusion
  22.3 0.1 copy.32
  22.4 20.5 %all_gather.3 = bf16[32,2048]{1,0:T(8,128)(2,1)S(1)} all-gather(bf16[32,128]{1,0:T(8,128)(2,1)} %param.14), channel_id=1, replica_groups=mesh['wide'=16,'long'=16] {'wide'}, dimensions={1}, use_global_device_ids=true | all-gather | bytes 139264 | tf_op jit(solution)/shard_map/all_gather | solution.py:85
  43.0 0.0 copy-done
  43.1 0.0 all-to-all-done
  43.1 19.3 %multiply_convert_fusion.1 = (bf16[512,2048]{1,0:T(8,128)(2,1)S(1)}, bf16[512,2048]{1,0:T(8,128)(2,1)S(1)}) fusion(f32[2048]{0:T(1024)S(1)} %bitcast.61, f32[512]{0:T(512)S(1)} %bitcast.65, f32[2048]{0:T(1024)S(1)} %bitcast.62, f32[512]{0:T(512)S(1)} %bitcast.66, f32[2048]{0:T(1024)S(1)} %bitcast.63, f32[512]{0:T(512)S(1)} %bitcast.64, ...), kind=kLoop, calls=%fused_computation.15 | loop fusion | flops 20971520 | bytes 4235264 | tf_op jit(solution)/shard_map/convert_element_type | solution.py:38
  62.4 1.3 copy-done.1
  63.7 1.9 fusion.8
  65.7 0.0 reduce-scatter.7.cloned.1.call-update
  65.7 0.0 reduce-scatter.5.cloned.1.call-start
  65.8 3.1 %fusion.4 = f32[32,2048]{1,0:T(8,128)} fusion(bf16[512,2048]{1,0:T(8,128)(2,1)} %copy-done.1, bf16[512,2048]{1,0:T(8,128)(2,1)S(1)} %get-tuple-element.13, bf16[16,512]{1,0:T(8,128)(2,1)S(1)} %get-tuple-element.16, bf16[16,512]{1,0:T(8,128)(2,1)S(1)} %get-tuple-element.17, bf16[16,512]{1,0:T(8,128)(2,1)S(1)} %get-tuple-element.15), kind=kOutput, calls=%fused_computation.10 | convolution fusion | flops 142868480 | bytes 4505600 | tf_op jit(solution)/shard_map/dot_general | solution.py:70
  68.9 0.0 reduce-scatter.5.cloned.1.call-update
  68.9 81.1 %reduce-scatter.7.cloned.1.call-done = f32[32,32]{1,0:T(8,128)} async-done(((f32[512,32]{1,0:T(8,128)}), f32[32,32]{1,0:T(8,128)}) %reduce-scatter.7.cloned.1.call-update) | async-done | bytes 4112
  150.0 1.4 copy.44
  151.4 62.9 %reduce-scatter.5.cloned.1.call-done = f32[32,128]{1,0:T(8,128)} async-done(((f32[32,2048]{1,0:T(8,128)}), f32[32,128]{1,0:T(8,128)}) %reduce-scatter.5.cloned.1.call-update) | async-done | bytes 16400 | tf_op jit(solution)/shard_map/reduce_scatter | solution.py:90
  (23 shorter events, 0.2 us)
Async XLA Ops:
  7.2 35.8 %copy-start = (bf16[32,512]{1,0:T(8,128)(2,1)S(1)}, bf16[32,512]{1,0:T(8,128)(2,1)}, u32[]{:S(2)}) copy-start(bf16[32,512]{1,0:T(8,128)(2,1)} %param.15) | copy-start | bytes 98308
  11.5 31.6 %all-to-all-start = ((f32[16,4,128]{2,1,0:T(4,128)}), f32[16,4,128]{2,1,0:T(4,128)S(1)}, u32[]{:S(2)}, u32[]{:S(2)}) async-start(f32[16,4,128]{2,1,0:T(4,128)} %stack.2), calls=%async_computation | async-start | bytes 65536 | tf_op jit(solution)/shard_map/all_to_all | solution.py:83
  17.3 132.8 %reduce-scatter.7.cloned.1.call-start = ((), (), s32[]{:S(2)}) async-start(), calls=%async_computation.4 | async-start | bytes 278528
  62.4 1.3 copy-start.1
  65.7 148.6 %reduce-scatter.5.cloned.1.call-start = ((), (), s32[]{:S(2)}) async-start(), calls=%async_computation.3 | async-start | bytes 278528 | tf_op jit(solution)/shard_map/reduce_scatter | solution.py:90
Sparse Core Ops, SparseCore 0:
  65.8 84.1 reduce-scatter.6
  153.2 61.0 reduce-scatter.4
